TPU v7x, 32 devices: a whole 2x2x4 slice. The times are simulated.
32 devices in a mesh: tbl: 8 (over z, core), grp: 4 (over y, x).
Axes of the slice: x: 2, y: 2, z: 4, core: 2. Of those that a mesh axis runs over, the one named last changes fastest.
Arguments:
- codes: bfloat16 [8, 1024, 256], P('tbl', 'grp'), may hold values from -4 to 4
- row_scales: float32 [8, 1024], P('tbl', 'grp'), may hold values from 0.25 to 16
- history_lengths: int32 [32, 8], P(None, 'tbl'), may hold values from 1 to 32, as said below
- history_ids: int32 [32, 8, 32], P(None, 'tbl'), may hold values from 0 to 1023, as said below
- query_items: int32 [32, 8], P(None, 'tbl'), may hold values from 0 to 1023, as said below
- slot_tables: int32 [8], replicated, may hold values from 0 to 7, each once
Outputs:
- pooled: bfloat16 [32, 8, 256], P(('tbl', 'grp'))
Inputs may be any that keep to these rules, and one draw needn't show every extreme that they name: `history_lengths`: the largest length, 32, occurs in every draw. `history_ids`: entries at positions at or beyond the history's length are row ids too, and are to be ignored. query_items[b, s] equals history_ids[b, s, h] for some h below history_lengths[b, s].
All inputs are finite; a program needn't handle non-finite values.
Results may differ from a plain program's by a relative error of at most 0.004.
Values may be sent and summed in bfloat16 or wider, within the bound.
A program may use at most 64 MiB of HBM per device.

v0:
```python
import jax
import jax.numpy as jnp
from jax import lax
from jax.sharding import PartitionSpec as P


def combined_all(value, axis, combine):
    everything = jax.tree.map(lambda part: lax.all_gather(part, axis), value)
    leading = jax.tree.map(lambda part: part[0], everything)

    def hop(k, so_far):
        return combine(so_far, jax.tree.map(lambda part: part[k], everything))

    return lax.fori_loop(1, lax.axis_size(axis), hop, leading)


def combine(first, second):
    first_peak, first_mass, first_sums = first
    second_peak, second_mass, second_sums = second
    peak = jnp.maximum(first_peak, second_peak)
    first_factor = jnp.exp(first_peak - peak)
    second_factor = jnp.exp(second_peak - peak)
    return (
        peak,
        first_mass * first_factor + second_mass * second_factor,
        first_sums * first_factor[..., None] + second_sums * second_factor[..., None],
    )


def per_device(codes, row_scales, history_lengths, history_ids, query_items, slot_tables):
    slot_count, row_count, emb_width = codes.shape
    batch_rows, _, history = history_ids.shape
    tbl_count = lax.axis_size("tbl")
    grp_count = lax.axis_size("grp")
    owned_rows = batch_rows // (tbl_count * grp_count)
    grp_index = lax.axis_index("grp")
    offset = grp_index * row_count
    query_local = query_items - offset
    query_owned = (query_local >= 0) & (query_local < row_count)
    query_index = jnp.clip(query_local, 0, row_count - 1)
    found = jnp.take(codes[0], query_index[:, 0], axis=0).astype(jnp.float32)
    factor = jnp.take(row_scales[0], query_index[:, 0], axis=0)
    code_parts = [jnp.where(query_owned[:, 0, None], found, 0.0)]
    scale_parts = [jnp.where(query_owned[:, 0], factor, 0.0)]
    query_codes = jnp.stack(code_parts, axis=1)
    query_scales = jnp.stack(scale_parts, axis=1)
    query = lax.psum((query_codes * query_scales[..., None]).astype(jnp.bfloat16), "grp").astype(
        jnp.float32
    )
    positions = jnp.arange(history, dtype=jnp.int32)
    row_iota = jnp.arange(row_count, dtype=jnp.int32)
    table_rows = codes.astype(jnp.float32)
    block_count = 8
    block_rows = batch_rows // block_count

    def partial_value(block):
        block_ids, block_lengths, block_query = block
        local = block_ids - offset
        live = positions[None, None, :] < block_lengths[:, :, None]
        local = jnp.where(live, local, -1)
        peaks, masses, sums = ([], [], [])
        rows_f = table_rows[0]
        factor = row_scales[0]
        counts = jnp.sum(
            (local[:, 0, :, None] == row_iota[None, None, :]).astype(jnp.float32), axis=1
        )
        raw = jnp.dot(block_query[:, 0], rows_f.T, precision=lax.Precision.HIGHEST)
        score = raw * factor[None, :] / emb_width
        named = counts > 0.0
        peak = jnp.max(jnp.where(named, score, -1e30), axis=1)
        weight = jnp.where(
            named,
            counts * jnp.exp(jnp.where(named, score, 0.0) - jnp.where(named, peak[:, None], 0.0)),
            0.0,
        )
        peaks.append(peak)
        masses.append(jnp.sum(weight, axis=1))
        sums.append(jnp.dot(weight * factor[None, :], rows_f, precision=lax.Precision.HIGHEST))
        return (jnp.stack(peaks, axis=1), jnp.stack(masses, axis=1), jnp.stack(sums, axis=1))

    block_peaks, block_masses, block_sums = lax.map(
        partial_value,
        (
            history_ids.reshape(block_count, block_rows, slot_count, history),
            history_lengths.reshape(block_count, block_rows, slot_count),
            query.reshape(block_count, block_rows, slot_count, emb_width),
        ),
    )
    lead = (tbl_count, grp_count, owned_rows)
    peaks = block_peaks.reshape(lead + (slot_count,))
    masses = block_masses.reshape(lead + (slot_count,))
    sums = block_sums.reshape(lead + (slot_count, emb_width))
    all_peak, all_mass, all_sums = combined_all((peaks, masses, sums), "grp", combine)
    mass = lax.dynamic_index_in_dim(all_mass, grp_index, 1, keepdims=False)
    weighted = lax.dynamic_index_in_dim(all_sums, grp_index, 1, keepdims=False)
    pooled_slot = (weighted / mass[..., None]).astype(jnp.bfloat16)
    outgoing = jnp.transpose(pooled_slot, (1, 0, 2, 3))
    arrived = lax.all_to_all(outgoing, "tbl", split_axis=1, concat_axis=1, tiled=True)
    arranged = arrived.reshape(owned_rows, tbl_count * slot_count, emb_width)
    inverse = jnp.argsort(slot_tables)
    return jnp.take(arranged, inverse, axis=1)


def solution(mesh):
    placed = (
        P("tbl", "grp", None),
        P("tbl", "grp"),
        P(None, "tbl"),
        P(None, "tbl", None),
        P(None, "tbl"),
        P(),
    )
    return jax.shard_map(
        per_device,
        mesh=mesh,
        in_specs=placed,
        out_specs=P(("tbl", "grp"), None, None),
        check_vma=False,
    )
```

profile of v0, /device:TPU:0, one launch (start us, length us, event | category | flops | bytes accessed | tf_op | source)
XLA Modules:
  0.0 74.8 jit_solution(50232354431573683)
XLA Ops:
  0.0 0.7 copy-done.2
  0.7 0.7 copy-done
  1.4 0.7 gather_fusion.1
  3.0 17.8 %psum.7 = bf16[8,4,1,256]{3,2,1,0:T(2,128)(2,1)S(1)} all-reduce(bf16[8,4,1,256]{3,2,1,0:T(2,128)(2,1)S(1)} %reshape.329), channel_id=1, replica_groups=mesh['tbl'=8,'grp'=4] {'grp'}, use_global_device_ids=true, to_apply=%region_1.2 | all-reduce | flops 8192 | bytes 32768 | tf_op jit(solution)/shard_map/psum | solution.py:47
  21.5 0.7 reduce.3
  22.3 14.2 %while.35 = (s32[]{:T(128)}, f32[8,4,1]{1,2,0:T(1,128)S(1)}, f32[8,4,1]{1,2,0:T(1,128)S(1)}, f32[8,4,1,256]{3,1,2,0:T(4,128)S(1)}, s32[8,4,1]{1,2,0:T(1,128)S(1)...) while((s32[]{:T(128)}, f32[8,4,1]{1,2,0:T(1,128)S(1)}, ...), condition=%wide.region_6.7_spmd.clone, body=%wide.region_2.6_spmd.clone.sunk | while | flops 6402426 | bytes 575205 | solution.py:81
  22.3 0.8 %bitcast_select_fusion.4 = s32[4,32]{1,0:T(4,128)S(1)} fusion(s32[8,4,1,32]{3,1,2,0:T(4,128)} %get-tuple-element.560, s32[]{:T(128)} %get-tuple-element.544, s32[]{:T(128)} %get-tuple-element.561, s32[4]{0:T(128)S(1)} %fusion.37), kind=kLoop, calls=%fused_computation.31.clone.1 | loop fusion | flops 384 | bytes 1048 | tf_op jit(solution)/shard_map/while/body/eval_jaxpr/jit(_where)/select_n | solution.py:60
  24.0 0.8 %bitcast_select_fusion.4 = s32[4,32]{1,0:T(4,128)S(1)} fusion(s32[8,4,1,32]{3,1,2,0:T(4,128)} %get-tuple-element.560, s32[]{:T(128)} %get-tuple-element.544, s32[]{:T(128)} %get-tuple-element.561, s32[4]{0:T(128)S(1)} %fusion.37), kind=kLoop, calls=%fused_computation.31.clone.1 | loop fusion | flops 384 | bytes 1048 | tf_op jit(solution)/shard_map/while/body/eval_jaxpr/jit(_where)/select_n | solution.py:60
  25.8 0.8 %bitcast_select_fusion.4 = s32[4,32]{1,0:T(4,128)S(1)} fusion(s32[8,4,1,32]{3,1,2,0:T(4,128)} %get-tuple-element.560, s32[]{:T(128)} %get-tuple-element.544, s32[]{:T(128)} %get-tuple-element.561, s32[4]{0:T(128)S(1)} %fusion.37), kind=kLoop, calls=%fused_computation.31.clone.1 | loop fusion | flops 384 | bytes 1048 | tf_op jit(solution)/shard_map/while/body/eval_jaxpr/jit(_where)/select_n | solution.py:60
  27.6 0.8 %bitcast_select_fusion.4 = s32[4,32]{1,0:T(4,128)S(1)} fusion(s32[8,4,1,32]{3,1,2,0:T(4,128)} %get-tuple-element.560, s32[]{:T(128)} %get-tuple-element.544, s32[]{:T(128)} %get-tuple-element.561, s32[4]{0:T(128)S(1)} %fusion.37), kind=kLoop, calls=%fused_computation.31.clone.1 | loop fusion | flops 384 | bytes 1048 | tf_op jit(solution)/shard_map/while/body/eval_jaxpr/jit(_where)/select_n | solution.py:60
  29.4 0.8 %bitcast_select_fusion.4 = s32[4,32]{1,0:T(4,128)S(1)} fusion(s32[8,4,1,32]{3,1,2,0:T(4,128)} %get-tuple-element.560, s32[]{:T(128)} %get-tuple-element.544, s32[]{:T(128)} %get-tuple-element.561, s32[4]{0:T(128)S(1)} %fusion.37), kind=kLoop, calls=%fused_computation.31.clone.1 | loop fusion | flops 384 | bytes 1048 | tf_op jit(solution)/shard_map/while/body/eval_jaxpr/jit(_where)/select_n | solution.py:60
  31.2 0.8 %bitcast_select_fusion.4 = s32[4,32]{1,0:T(4,128)S(1)} fusion(s32[8,4,1,32]{3,1,2,0:T(4,128)} %get-tuple-element.560, s32[]{:T(128)} %get-tuple-element.544, s32[]{:T(128)} %get-tuple-element.561, s32[4]{0:T(128)S(1)} %fusion.37), kind=kLoop, calls=%fused_computation.31.clone.1 | loop fusion | flops 384 | bytes 1048 | tf_op jit(solution)/shard_map/while/body/eval_jaxpr/jit(_where)/select_n | solution.py:60
  33.0 0.8 %bitcast_select_fusion.4 = s32[4,32]{1,0:T(4,128)S(1)} fusion(s32[8,4,1,32]{3,1,2,0:T(4,128)} %get-tuple-element.560, s32[]{:T(128)} %get-tuple-element.544, s32[]{:T(128)} %get-tuple-element.561, s32[4]{0:T(128)S(1)} %fusion.37), kind=kLoop, calls=%fused_computation.31.clone.1 | loop fusion | flops 384 | bytes 1048 | tf_op jit(solution)/shard_map/while/body/eval_jaxpr/jit(_where)/select_n | solution.py:60
  34.7 0.8 %bitcast_select_fusion.4 = s32[4,32]{1,0:T(4,128)S(1)} fusion(s32[8,4,1,32]{3,1,2,0:T(4,128)} %get-tuple-element.560, s32[]{:T(128)} %get-tuple-element.544, s32[]{:T(128)} %get-tuple-element.561, s32[4]{0:T(128)S(1)} %fusion.37), kind=kLoop, calls=%fused_computation.31.clone.1 | loop fusion | flops 384 | bytes 1048 | tf_op jit(solution)/shard_map/while/body/eval_jaxpr/jit(_where)/select_n | solution.py:60
  36.5 7.5 %all-gather.2 = f32[32,4,1,256]{3,1,2,0:T(4,128)S(1)} all-gather(f32[8,4,1,256]{3,1,2,0:T(4,128)S(1)} %get-tuple-element.250), channel_id=4, replica_groups=mesh['tbl'=8,'grp'=4] {'grp'}, dimensions={0}, use_global_device_ids=true | all-gather | bytes 163840 | tf_op jit(solution)/shard_map/all_gather | solution.py:8
  44.1 8.1 %all-gather = f32[32,4,1]{1,2,0:T(1,128)S(1)} all-gather(f32[8,4,1]{1,2,0:T(1,128)S(1)} %get-tuple-element.248), channel_id=2, replica_groups=mesh['tbl'=8,'grp'=4] {'grp'}, dimensions={0}, use_global_device_ids=true | all-gather | bytes 640 | tf_op jit(solution)/shard_map/all_gather | solution.py:8
  52.3 7.3 %all-gather.1 = f32[32,4,1]{1,2,0:T(1,128)S(1)} all-gather(f32[8,4,1]{1,2,0:T(1,128)S(1)} %get-tuple-element.249), channel_id=3, replica_groups=mesh['tbl'=8,'grp'=4] {'grp'}, dimensions={0}, use_global_device_ids=true | all-gather | bytes 640 | tf_op jit(solution)/shard_map/all_gather | solution.py:8
  59.8 1.4 %while.34 = (s32[]{:T(128)}, f32[8,4,1,1]{0,1,3,2:T(4,128)S(1)}, f32[8,4,1,1]{0,1,3,2:T(4,128)S(1)}, f32[8,4,1,1,256]{4,3,2,1,0:T(1,128)S(1)}, f32[4,8,4,1,1]{1,...) while((s32[]{:T(128)}, f32[8,4,1,1]{0,1,3,2:T(4,128)S(1)}, ...), condition=%wide.region_8.9_spmd, body=%wide.region_7.8_spmd.sunk | while | flops 24805 | bytes 166427 | solution.py:14
  61.9 0.7 reduce.4
  63.1 4.9 %all-to-all-start = ((bf16[8,2,128]{2,1,0:T(2,128)(2,1)}), bf16[8,2,128]{2,1,0:T(2,128)(2,1)S(1)}, u32[]{:S(2)}, u32[]{:S(2)}) async-start(bf16[8,2,128]{2,1,0:T(2,128)(2,1)} %reshape.339), calls=%async_computation | async-start | bytes 8192 | tf_op jit(solution)/shard_map/all_to_all | solution.py:98
  68.0 0.6 copy-done.4
  68.7 1.0 %sort.17 = (s32[8]{0:T(128)}, s32[8]{0:T(128)S(1)}) sort(s32[8]{0:T(128)S(1)} %copy-done.4, s32[8]{0:T(128)S(1)} %iota.10), dimensions={0}, to_apply=%region_0.1 | sort | flops 24 | bytes 128 | tf_op jit(solution)/shard_map/jit(argsort)/sort | solution.py:100
  69.7 3.8 %all-to-all-done = bf16[8,2,128]{2,1,0:T(2,128)(2,1)S(1)} async-done(((bf16[8,2,128]{2,1,0:T(2,128)(2,1)}), bf16[8,2,128]{2,1,0:T(2,128)(2,1)S(1)}, u32[]{:S(2)}, u32[]{:S(2)}) %all-to-all-start) | async-done | bytes 4128 | tf_op jit(solution)/shard_map/all_to_all | solution.py:98
  74.1 0.7 bitcast_select_fusion.2
  (116 shorter events, 13.1 us)
Async XLA Ops:
  0.0 0.7 copy-start.2
  0.7 0.7 copy-start
  1.4 0.9 %copy-start.1 = (bf16[1,256,256]{2,1,0:T(8,128)(2,1)S(1)}, bf16[1,256,256]{2,1,0:T(8,128)(2,1)}, u32[]{:S(2)}) copy-start(bf16[1,256,256]{2,1,0:T(8,128)(2,1)} %param.10) | copy-start | bytes 393220
  20.9 0.7 copy-start.3
  63.1 10.4 %all-to-all-start = ((bf16[8,2,128]{2,1,0:T(2,128)(2,1)}), bf16[8,2,128]{2,1,0:T(2,128)(2,1)S(1)}, u32[]{:S(2)}, u32[]{:S(2)}) async-start(bf16[8,2,128]{2,1,0:T(2,128)(2,1)} %reshape.339), calls=%async_computation | async-start | bytes 8192 | tf_op jit(solution)/shard_map/all_to_all | solution.py:98
  68.0 0.7 copy-start.4
where the time goes:
time: 75.3 us; the launch traced here: 74.8 us
  blocking collectives  40.7 us (54%)
  other arithmetic  12.5 us (17%)
  local copies, waits for them, and re-layouts  7.25 us (10%)
  matrix products  5.05 us (7%)
  starting transfers between devices  4.88 us (6%)
  waiting for transfers between devices  3.79 us (5%)
    all_gather x3, blocking collectives, combined_all(): everything = jax.tree.map(lambda part: lax.all_gather(part, axis), value)  22.9 us
    psum x1, blocking collectives, per_device(): lax.psum((query_codes * query_scales[..., None]).astype(jnp.bfloat16), 'g...  17.8 us
    select_n x8, other arithmetic, partial_value(): local = jnp.where(live, local, -1)  6.06 us
    all_to_all x1, starting transfers between devices, per_device(): lax.all_to_all(outgoing, 'tbl', split_axis=1, concat_axis=1, tiled=True)  4.88 us
    unnamed x15, local copies, waits for them, and re-layouts  3.95 us
    all_to_all x1, waiting for transfers between devices, per_device(): lax.all_to_all(outgoing, 'tbl', split_axis=1, concat_axis=1, tiled=True)  3.79 us
    dot_general x8, matrix products, partial_value(): raw = jnp.dot(block_query[:, 0], rows_f.T, precision=lax.Precision.HIGHEST)  3.42 us
    dot_general x8, matrix products, partial_value(): jnp.dot(weight * factor[None, :], rows_f, precision=lax.Precision.HIGHEST)  1.63 us
  transfers between devices with their start and end apart: 1, of which 1 were waited for; matrix products, arithmetic and copies ran while one was open for 1% of the time, Pallas kernels for 0%

commit v1 on v0

--- a/solution.py
+++ b/solution.py
@@ -2,6 +2,11 @@
 import jax.numpy as jnp
 from jax import lax
 from jax.sharding import PartitionSpec as P
+
+
+def summed_here(block, axis):
+    parts = lax.all_gather(block, axis)
+    return jnp.sum(parts, axis=0)
 
 
 def combined_all(value, axis, combine):
@@ -44,7 +49,7 @@
     scale_parts = [jnp.where(query_owned[:, 0], factor, 0.0)]
     query_codes = jnp.stack(code_parts, axis=1)
     query_scales = jnp.stack(scale_parts, axis=1)
-    query = lax.psum((query_codes * query_scales[..., None]).astype(jnp.bfloat16), "grp").astype(
+    query = summed_here((query_codes * query_scales[..., None]).astype(jnp.bfloat16), "grp").astype(
         jnp.float32
     )
     positions = jnp.arange(history, dtype=jnp.int32)

time: 75.3 us -> 68.2 us (0.906)
  blocking collectives: 40.7 us -> 33.6 us
    psum x1 -> x0, blocking collectives: 17.8 us -> none  [per_device(): lax.psum((query_codes * query_scales[..., None]).astype(jnp.bfloat16), 'g...]
    all_gather x0 -> x1, blocking collectives: none -> 9.72 us  [summed_here(): parts = lax.all_gather(block, axis)]
    all_gather x3, blocking collectives: 22.9 us -> 23.8 us  [combined_all(): everything = jax.tree.map(lambda part: lax.all_gather(part, axis), value)]
  transfers between devices with their start and end apart: 1 -> 1, of which waited for: 1 -> 1; matrix products, arithmetic and copies ran while one was open for 1% -> 2% of each run, Pallas kernels for 0% -> 0%
where the time goes in v1:
time: 68.2 us; the launch traced here: 67.7 us
  blocking collectives  33.6 us (49%)
  other arithmetic  12.5 us (18%)
  local copies, waits for them, and re-layouts  7.28 us (11%)
  matrix products  5.05 us (7%)
  starting transfers between devices  4.88 us (7%)
  waiting for transfers between devices  3.79 us (6%)
    all_gather x3, blocking collectives, combined_all(): everything = jax.tree.map(lambda part: lax.all_gather(part, axis), value)  23.8 us
    all_gather x1, blocking collectives, summed_here(): parts = lax.all_gather(block, axis)  9.72 us
    select_n x8, other arithmetic, partial_value(): local = jnp.where(live, local, -1)  6.06 us
    all_to_all x1, starting transfers between devices, per_device(): lax.all_to_all(outgoing, 'tbl', split_axis=1, concat_axis=1, tiled=True)  4.88 us
    unnamed x15, local copies, waits for them, and re-layouts  3.95 us
    all_to_all x1, waiting for transfers between devices, per_device(): lax.all_to_all(outgoing, 'tbl', split_axis=1, concat_axis=1, tiled=True)  3.79 us
    dot_general x8, matrix products, partial_value(): raw = jnp.dot(block_query[:, 0], rows_f.T, precision=lax.Precision.HIGHEST)  3.42 us
    dot_general x8, matrix products, partial_value(): jnp.dot(weight * factor[None, :], rows_f, precision=lax.Precision.HIGHEST)  1.63 us
  transfers between devices with their start and end apart: 1, of which 1 were waited for; matrix products, arithmetic and copies ran while one was open for 2% of the time, Pallas kernels for 0%

profile of v1, /device:TPU:0, one launch (start us, length us, event | category | flops | bytes accessed | tf_op | source)
XLA Modules:
  0.0 67.7 jit_solution(5976676111412366025)
XLA Ops:
  0.0 0.7 copy-done.2
  0.7 0.7 copy-done
  1.4 0.7 %gather_fusion.1 = f32[32]{0:T(128)S(1)} fusion(f32[256]{0:T(256)S(1)} %bitcast.113, s32[1024]{0:T(1024)S(1)} %pad_clamp_fusion.1), kind=kCustom, calls=%fused_computation.1 | custom fusion | bytes 384 | tf_op jit(solution)/shard_map/jit(_take)/gather | solution.py:47
  3.0 9.7 %all_gather.13 = bf16[4,32,1,256]{3,1,2,0:T(8,128)(2,1)S(1)} all-gather(bf16[1,32,1,256]{3,1,2,0:T(8,128)(2,1)S(1)} %multiply_convert_fusion), channel_id=1, replica_groups=mesh['tbl'=8,'grp'=4] {'grp'}, dimensions={0}, use_global_device_ids=true | all-gather | bytes 81920 | tf_op jit(solution)/shard_map/all_gather | solution.py:8
  13.5 0.7 reduce.5
  14.2 14.2 %while.35 = (s32[]{:T(128)}, f32[8,4,1]{1,2,0:T(1,128)S(1)}, f32[8,4,1]{1,2,0:T(1,128)S(1)}, f32[8,4,1,256]{3,1,2,0:T(4,128)S(1)}, s32[8,4,1]{1,2,0:T(1,128)S(1)...) while((s32[]{:T(128)}, f32[8,4,1]{1,2,0:T(1,128)S(1)}, ...), condition=%wide.region_6.7_spmd.clone, body=%wide.region_2.6_spmd.clone.sunk | while | flops 6402426 | bytes 575205 | solution.py:86
  14.2 0.8 %bitcast_select_fusion.4 = s32[4,32]{1,0:T(4,128)S(1)} fusion(s32[8,4,1,32]{3,1,2,0:T(4,128)} %get-tuple-element.560, s32[]{:T(128)} %get-tuple-element.544, s32[]{:T(128)} %get-tuple-element.561, s32[4]{0:T(128)S(1)} %fusion.37), kind=kLoop, calls=%fused_computation.31.clone.1 | loop fusion | flops 384 | bytes 1048 | tf_op jit(solution)/shard_map/while/body/eval_jaxpr/jit(_where)/select_n | solution.py:65
  16.0 0.8 %bitcast_select_fusion.4 = s32[4,32]{1,0:T(4,128)S(1)} fusion(s32[8,4,1,32]{3,1,2,0:T(4,128)} %get-tuple-element.560, s32[]{:T(128)} %get-tuple-element.544, s32[]{:T(128)} %get-tuple-element.561, s32[4]{0:T(128)S(1)} %fusion.37), kind=kLoop, calls=%fused_computation.31.clone.1 | loop fusion | flops 384 | bytes 1048 | tf_op jit(solution)/shard_map/while/body/eval_jaxpr/jit(_where)/select_n | solution.py:65
  17.8 0.8 %bitcast_select_fusion.4 = s32[4,32]{1,0:T(4,128)S(1)} fusion(s32[8,4,1,32]{3,1,2,0:T(4,128)} %get-tuple-element.560, s32[]{:T(128)} %get-tuple-element.544, s32[]{:T(128)} %get-tuple-element.561, s32[4]{0:T(128)S(1)} %fusion.37), kind=kLoop, calls=%fused_computation.31.clone.1 | loop fusion | flops 384 | bytes 1048 | tf_op jit(solution)/shard_map/while/body/eval_jaxpr/jit(_where)/select_n | solution.py:65
  19.5 0.8 %bitcast_select_fusion.4 = s32[4,32]{1,0:T(4,128)S(1)} fusion(s32[8,4,1,32]{3,1,2,0:T(4,128)} %get-tuple-element.560, s32[]{:T(128)} %get-tuple-element.544, s32[]{:T(128)} %get-tuple-element.561, s32[4]{0:T(128)S(1)} %fusion.37), kind=kLoop, calls=%fused_computation.31.clone.1 | loop fusion | flops 384 | bytes 1048 | tf_op jit(solution)/shard_map/while/body/eval_jaxpr/jit(_where)/select_n | solution.py:65
  21.3 0.8 %bitcast_select_fusion.4 = s32[4,32]{1,0:T(4,128)S(1)} fusion(s32[8,4,1,32]{3,1,2,0:T(4,128)} %get-tuple-element.560, s32[]{:T(128)} %get-tuple-element.544, s32[]{:T(128)} %get-tuple-element.561, s32[4]{0:T(128)S(1)} %fusion.37), kind=kLoop, calls=%fused_computation.31.clone.1 | loop fusion | flops 384 | bytes 1048 | tf_op jit(solution)/shard_map/while/body/eval_jaxpr/jit(_where)/select_n | solution.py:65
  23.1 0.8 %bitcast_select_fusion.4 = s32[4,32]{1,0:T(4,128)S(1)} fusion(s32[8,4,1,32]{3,1,2,0:T(4,128)} %get-tuple-element.560, s32[]{:T(128)} %get-tuple-element.544, s32[]{:T(128)} %get-tuple-element.561, s32[4]{0:T(128)S(1)} %fusion.37), kind=kLoop, calls=%fused_computation.31.clone.1 | loop fusion | flops 384 | bytes 1048 | tf_op jit(solution)/shard_map/while/body/eval_jaxpr/jit(_where)/select_n | solution.py:65
  24.9 0.8 %bitcast_select_fusion.4 = s32[4,32]{1,0:T(4,128)S(1)} fusion(s32[8,4,1,32]{3,1,2,0:T(4,128)} %get-tuple-element.560, s32[]{:T(128)} %get-tuple-element.544, s32[]{:T(128)} %get-tuple-element.561, s32[4]{0:T(128)S(1)} %fusion.37), kind=kLoop, calls=%fused_computation.31.clone.1 | loop fusion | flops 384 | bytes 1048 | tf_op jit(solution)/shard_map/while/body/eval_jaxpr/jit(_where)/select_n | solution.py:65
  26.7 0.8 %bitcast_select_fusion.4 = s32[4,32]{1,0:T(4,128)S(1)} fusion(s32[8,4,1,32]{3,1,2,0:T(4,128)} %get-tuple-element.560, s32[]{:T(128)} %get-tuple-element.544, s32[]{:T(128)} %get-tuple-element.561, s32[4]{0:T(128)S(1)} %fusion.37), kind=kLoop, calls=%fused_computation.31.clone.1 | loop fusion | flops 384 | bytes 1048 | tf_op jit(solution)/shard_map/while/body/eval_jaxpr/jit(_where)/select_n | solution.py:65
  28.4 8.5 %all-gather.2 = f32[32,4,1,256]{3,1,2,0:T(4,128)S(1)} all-gather(f32[8,4,1,256]{3,1,2,0:T(4,128)S(1)} %get-tuple-element.250), channel_id=4, replica_groups=mesh['tbl'=8,'grp'=4] {'grp'}, dimensions={0}, use_global_device_ids=true | all-gather | bytes 163840 | tf_op jit(solution)/shard_map/all_gather | solution.py:13
  37.0 7.2 %all-gather = f32[32,4,1]{1,2,0:T(1,128)S(1)} all-gather(f32[8,4,1]{1,2,0:T(1,128)S(1)} %get-tuple-element.248), channel_id=2, replica_groups=mesh['tbl'=8,'grp'=4] {'grp'}, dimensions={0}, use_global_device_ids=true | all-gather | bytes 640 | tf_op jit(solution)/shard_map/all_gather | solution.py:13
  44.3 8.2 %all-gather.1 = f32[32,4,1]{1,2,0:T(1,128)S(1)} all-gather(f32[8,4,1]{1,2,0:T(1,128)S(1)} %get-tuple-element.249), channel_id=3, replica_groups=mesh['tbl'=8,'grp'=4] {'grp'}, dimensions={0}, use_global_device_ids=true | all-gather | bytes 640 | tf_op jit(solution)/shard_map/all_gather | solution.py:13
  52.7 1.4 %while.34 = (s32[]{:T(128)}, f32[8,4,1,1]{0,1,3,2:T(4,128)S(1)}, f32[8,4,1,1]{0,1,3,2:T(4,128)S(1)}, f32[8,4,1,1,256]{4,3,2,1,0:T(1,128)S(1)}, f32[4,8,4,1,1]{1,...) while((s32[]{:T(128)}, f32[8,4,1,1]{0,1,3,2:T(4,128)S(1)}, ...), condition=%wide.region_8.9_spmd, body=%wide.region_7.8_spmd.sunk | while | flops 24805 | bytes 166427 | solution.py:19
  54.7 0.7 reduce.6
  56.0 4.9 %all-to-all-start = ((bf16[8,2,128]{2,1,0:T(2,128)(2,1)}), bf16[8,2,128]{2,1,0:T(2,128)(2,1)S(1)}, u32[]{:S(2)}, u32[]{:S(2)}) async-start(bf16[8,2,128]{2,1,0:T(2,128)(2,1)} %reshape.352), calls=%async_computation | async-start | bytes 8192 | tf_op jit(solution)/shard_map/all_to_all | solution.py:103
  60.9 0.6 copy-done.4
  61.5 1.0 %sort.17 = (s32[8]{0:T(128)}, s32[8]{0:T(128)S(1)}) sort(s32[8]{0:T(128)S(1)} %copy-done.4, s32[8]{0:T(128)S(1)} %iota.10), dimensions={0}, to_apply=%region_0.1 | sort | flops 24 | bytes 128 | tf_op jit(solution)/shard_map/jit(argsort)/sort | solution.py:105
  62.6 3.8 %all-to-all-done = bf16[8,2,128]{2,1,0:T(2,128)(2,1)S(1)} async-done(((bf16[8,2,128]{2,1,0:T(2,128)(2,1)}), bf16[8,2,128]{2,1,0:T(2,128)(2,1)S(1)}, u32[]{:S(2)}, u32[]{:S(2)}) %all-to-all-start) | async-done | bytes 4128 | tf_op jit(solution)/shard_map/all_to_all | solution.py:103
  67.0 0.7 bitcast_select_fusion.2
  (116 shorter events, 13.1 us)
Async XLA Ops:
  0.0 0.7 copy-start.2
  0.7 0.7 %copy-start = (f32[1,256]{1,0:T(1,128)S(1)}, f32[1,256]{1,0:T(1,128)}, u32[]{:S(2)}) copy-start(f32[1,256]{1,0:T(1,128)} %param.11) | copy-start | bytes 3076
  1.4 0.9 %copy-start.1 = (bf16[1,256,256]{2,1,0:T(8,128)(2,1)S(1)}, bf16[1,256,256]{2,1,0:T(8,128)(2,1)}, u32[]{:S(2)}) copy-start(bf16[1,256,256]{2,1,0:T(8,128)(2,1)} %param.10) | copy-start | bytes 393220
  12.8 0.7 copy-start.3
  56.0 10.4 %all-to-all-start = ((bf16[8,2,128]{2,1,0:T(2,128)(2,1)}), bf16[8,2,128]{2,1,0:T(2,128)(2,1)S(1)}, u32[]{:S(2)}, u32[]{:S(2)}) async-start(bf16[8,2,128]{2,1,0:T(2,128)(2,1)} %reshape.352), calls=%async_computation | async-start | bytes 8192 | tf_op jit(solution)/shard_map/all_to_all | solution.py:103
  60.9 0.7 copy-start.4
